TPU v7x, 32 devices: a whole 2x2x4 slice. The times are simulated.
32 devices in a mesh: blk: 8 (over y, x, core), wide: 4 (over z).
Axes of the slice: x: 2, y: 2, z: 4, core: 2. Of those that a mesh axis runs over, the one named last changes fastest.
Arguments:
- coupling: bfloat16 [1024, 8, 2, 512], P('blk', 'wide'), may hold values from -0.09375 to 0.09375
- rp_cells: int32 [3, 1024], replicated, may hold values from -8 to 7
- re_cells: int32 [3, 8], P(None, 'wide'), may hold values from -8 to 7
- q_points: int32 [3, 2048], P(None, 'blk'), may hold values from 0 to 31
- k_points: int32 [3, 2], replicated, may hold values from 0 to 31
- mode_energy: float32 [16, 2048], P(None, 'blk'), may hold values from 0.02 to 1
Outputs:
- bloch_coupling: float32 [2, 2, 512, 2048], P(None, None, 'wide', 'blk')
All inputs are finite; a program needn't handle non-finite values.
Results may differ from a plain program's by a relative error of at most 0.002.
Values may be sent and summed in bfloat16 or wider, within the bound.
No kernel may reach another device: no remote copies, remote signals or barrier semaphores. Data moves between devices by JAX's collectives and lax.ppermute only.
A program may use at most 64 MiB of HBM per device.

v0:
```python
import math
import jax
import jax.numpy as jnp
from jax import lax
from jax.sharding import PartitionSpec as P

MODES = 16
MESHQ = 32
MESHK = 32


def phase_parts(left, right, modulus):
    whole = jnp.sum(left[:, :, None] * right[:, None, :], axis=0)
    angle = jnp.mod(whole, modulus).astype(jnp.float32) * (2.0 * math.pi / modulus)
    return (jnp.cos(angle), jnp.sin(angle))


def q_table(q_points, vectors):
    cosine, sine = phase_parts(q_points, vectors, MESHQ)
    return jnp.concatenate([cosine, sine], axis=0).astype(jnp.bfloat16)


def entry_weights(mode_energy, offset, entries):
    weight = 1.0 / jnp.sqrt(2.0 * mode_energy)
    entry_index = offset + jnp.arange(entries, dtype=jnp.int32)
    selector = (
        (entry_index % MODES)[:, None] == jnp.arange(MODES, dtype=jnp.int32)[None, :]
    ).astype(jnp.float32)
    return jnp.dot(selector, weight, precision=lax.Precision.HIGHEST)


def on_device(coupling, rp_cells, re_cells, q_points, k_points, mode_energy):
    slab_rows = coupling.shape[0]
    q_local = q_points.shape[1]
    high = lax.Precision.HIGHEST
    moved = lax.all_to_all(coupling, "wide", split_axis=3, concat_axis=1, tiled=True)
    cells = lax.all_gather(re_cells, "wide", axis=1, tiled=True)
    entries = moved.shape[3]
    offset = lax.axis_index("wide") * entries
    cell_count = moved.shape[1]
    flat = moved.reshape(slab_rows, cell_count * 2 * entries)
    table = q_table(q_points, rp_cells)
    summed = lax.dot_general(
        lax.all_gather(flat, "blk", axis=0, tiled=True),
        table,
        (((0,), (1,)), ((), ())),
        preferred_element_type=jnp.float32,
    )
    summed = summed.reshape(cell_count, 2, entries, 2, q_local)
    real = summed[:, 0, :, 0] - summed[:, 1, :, 1]
    imag = summed[:, 1, :, 0] + summed[:, 0, :, 1]
    entry_weight = entry_weights(mode_energy, offset, entries)
    real = real * entry_weight[None]
    imag = imag * entry_weight[None]
    k_cos, k_sin = phase_parts(k_points, cells, MESHK)
    part_re = jnp.einsum("kr,req->keq", k_cos, real, precision=high) - jnp.einsum(
        "kr,req->keq", k_sin, imag, precision=high
    )
    part_im = jnp.einsum("kr,req->keq", k_cos, imag, precision=high) + jnp.einsum(
        "kr,req->keq", k_sin, real, precision=high
    )
    partial_value = jnp.stack([part_re, part_im], axis=1)
    return partial_value


def solution(mesh):
    in_specs = (
        P("blk", "wide", None, None),
        P(),
        P(None, "wide"),
        P(None, "blk"),
        P(),
        P(None, "blk"),
    )
    out_specs = P(None, None, "wide", "blk")
    return jax.shard_map(
        on_device, mesh=mesh, in_specs=in_specs, out_specs=out_specs, check_vma=False
    )
```

profile of v0, /device:TPU:0, one launch (start us, length us, event | category | flops | bytes accessed | tf_op | source)
XLA Modules:
  0.0 106.6 jit_solution(10636870011201941082)
XLA Ops:
  6.5 0.0 all-gather.3.cloned.1.call-start
  6.6 2.4 %copy.42 = bf16[128,2,2,512]{0,2,1,3:T(2,128)(2,1)S(1)} copy(bf16[128,2,2,512]{3,2,1,0:T(2,128)(2,1)} %param.6) | data formatting | bytes 1048576 | tf_op args[0]
  9.0 20.6 %all_to_all.15 = bf16[128,2,2,512]{0,2,1,3:T(2,128)(2,1)S(1)} all-to-all(bf16[128,2,2,512]{0,2,1,3:T(2,128)(2,1)S(1)} %copy.42), channel_id=1, replica_groups=mesh['blk'=8,'wide'=4] {'wide'}, dimensions={3} | all-to-all | bytes 1048576 | tf_op jit(solution)/shard_map/all_to_all | solution.py:36
  29.6 0.1 copy.43
  29.7 0.8 copy.44
  30.5 0.0 all-gather.3.cloned.1.call-update
  30.5 0.0 copy-done.4
  30.5 9.0 %all-gather = s32[4,2,3]{2,1,0:T(2,128)S(1)} all-gather(s32[1,2,3]{2,1,0:T(2,128)S(1)} %bitcast.40), channel_id=1, replica_groups=mesh['blk'=8,'wide'=4] {'wide'}, dimensions={0}, use_global_device_ids=true | all-gather | bytes 120 | tf_op jit(solution)/shard_map/all_gather | solution.py:37
  39.6 0.1 copy.41
  39.7 0.0 copy-done.5
  39.7 0.1 copy.40
  39.8 0.1 multiply_reduce_fusion.1
  39.8 0.1 fusion.25
  40.0 0.0 copy-done.1
  40.0 0.0 copy-done.3
  40.0 0.3 multiply_reduce_fusion
  40.3 0.3 fusion.10
  40.5 4.2 %cosine_convert_fusion = (bf16[256,1024]{1,0:T(8,128)(2,1)S(1)}, bf16[256,1024]{1,0:T(8,128)(2,1)S(1)}) fusion(s32[256,1024]{1,0:T(8,128)S(1)} %multiply_reduce_fusion), kind=kLoop, calls=%fused_computation.18 | loop fusion | flops 3932160 | bytes 2097152 | tf_op jit(solution)/shard_map/convert
  44.8 22.4 %all-gather.3.cloned.1.call-done = bf16[1024,2048]{0,1:T(8,128)(2,1)} async-done(((bf16[128,2048]{0,1:T(8,128)(2,1)}), bf16[1024,2048]{0,1:T(8,128)(2,1)}) %all-gather.3.cloned.1.call-update) | async-done | bytes 4194320 | tf_op jit(solution)/shard_map/all_gather | solution.py:44
  67.1 6.5 %convolution_bitcast_fusion = f32[2048,512]{0,1:T(8,128)} fusion(bf16[1024,2048]{0,1:T(8,128)(2,1)} %all-gather.3.cloned.1.call-done, bf16[256,1024]{1,0:T(8,128)(2,1)S(1)} %get-tuple-element.12, bf16[256,1024]{1,0:T(8,128)(2,1)S(1)} %get-tuple-element.11), kind=kOutput, calls=%fused_computation | convolution fusion | flops 2149580800 | bytes 9437184 | tf_op jit(solution)/shard_map/dot_general | solution.py:43
  73.7 6.6 %reshape.30 = f32[8,2,128,2,256]{2,1,0,4,3:T(2,128)} reshape(f32[2048,512]{0,1:T(8,128)} %convolution_bitcast_fusion) | data formatting | bytes 8388608 | tf_op jit(solution)/shard_map/reshape | solution.py:49
  80.3 8.1 %fusion.27 = (f32[8,1,128,1,256]{2,1,0,4,3:T(1,128)S(1)}, f32[8,1,128,1,256]{2,1,0,4,3:T(1,128)}, f32[8,1,128,1,256]{2,1,0,4,3:T(1,128)S(1)}, f32[8,1,128,1,256]{2,1,0,4,3:T(1,128)}) fusion(f32[8,2,128,2,256]{2,1,0,4,3:T(2,128)} %reshape.30), kind=kLoop, calls=%fused_computation.46 | loop fusion | bytes 8388608 | tf_op jit(solution)/shard_map/slice | solution.py:50
  88.4 0.6 copy.50
  89.0 0.6 copy.51
  89.6 1.6 %copy.52 = f32[8,1,128,1,256]{4,0,2,3,1:T(8,128)S(1)} copy(f32[8,1,128,1,256]{2,1,0,4,3:T(1,128)} %get-tuple-element.8) | data formatting | bytes 2097152
  91.2 2.3 %copy.53 = f32[8,1,128,1,256]{4,0,2,3,1:T(8,128)} copy(f32[8,1,128,1,256]{2,1,0,4,3:T(1,128)} %get-tuple-element.10) | data formatting | bytes 2097152
  93.5 1.0 fusion.8
  94.5 2.2 %fusion.9 = f32[2,128,256]{2,0,1:T(2,128)S(1)} fusion(f32[8,1,128,1,256]{4,0,2,3,1:T(8,128)S(1)} %copy.52, f32[8,1,128,1,256]{4,0,2,3,1:T(8,128)} %copy.53, f32[128,256]{1,0:T(8,128)S(1)} %fusion.10, f32[2,8]{1,0:T(2,128)S(1)} %cos.6), kind=kOutput, calls=%fused_computation.21 | convolution fusion | flops 6815744 | bytes 2490432 | tf_op jit(solution)/shard_map/kr,req->keq/dot_general | solution.py:59
  96.7 1.0 fusion.1
  97.7 1.0 fusion
  98.7 0.2 pad_maximum_fusion
  98.9 0.8 copy.49
  (10 shorter events, 0.1 us)
Async XLA Ops:
  6.5 24.0 %copy-start.4 = (s32[3,2]{0,1:T(2,128)S(1)}, s32[3,2]{0,1:T(2,128)}, u32[]{:S(2)}) copy-start(s32[3,2]{0,1:T(2,128)} %param.8) | copy-start | bytes 76
  6.5 33.1 %copy-start.5 = (s32[3,2]{0,1:T(2,128)S(1)}, s32[3,2]{0,1:T(2,128)}, u32[]{:S(2)}) copy-start(s32[3,2]{0,1:T(2,128)} %param.10) | copy-start | bytes 76
  6.5 33.4 %copy-start.1 = (s32[3,1024]{1,0:T(4,128)S(1)}, s32[3,1024]{1,0:T(4,128)}, u32[]{:S(2)}) copy-start(s32[3,1024]{1,0:T(4,128)} %param.7) | copy-start | bytes 36868
  6.5 33.4 %copy-start.3 = (s32[3,256]{1,0:T(4,128)S(1)}, s32[3,256]{1,0:T(4,128)}, u32[]{:S(2)}) copy-start(s32[3,256]{1,0:T(4,128)} %param.9) | copy-start | bytes 9220
  6.5 33.7 %copy-start.2 = (f32[16,256]{1,0:T(8,128)S(1)}, f32[16,256]{1,0:T(8,128)}, u32[]{:S(2)}) copy-start(f32[16,256]{1,0:T(8,128)} %param.11) | copy-start | bytes 49156
  6.5 60.6 %all-gather.3.cloned.1.call-start = ((), (), s32[]{:S(2)}) async-start(), calls=%async_computation.1 | async-start | bytes 4718592 | tf_op jit(solution)/shard_map/all_gather | solution.py:44
  93.5 3.2 %copy-start = (f32[8,1,128,1,256]{4,0,2,3,1:T(8,128)S(1)}, f32[8,1,128,1,256]{4,0,2,3,1:T(8,128)}, u32[]{:S(2)}) copy-start(f32[8,1,128,1,256]{4,0,2,3,1:T(8,128)} %copy.53) | copy-start | bytes 3145732
Sparse Core Ops, SparseCore 0:
  30.6 36.4 all-gather.2
where the time goes:
time: 107 us
  blocking collectives  29.7 us (28%)
  local copies, waits for them, and re-layouts  24.1 us (23%)
  waiting for transfers between devices  22.4 us (21%)
  between operations  13.6 us (13%)
  matrix products  12 us (11%)
  other arithmetic  4.91 us (5%)
    all_gather x1, waiting for transfers between devices, on_device(): lax.all_gather(flat, 'blk', axis=0, tiled=True)  22.4 us
    all_to_all x1, blocking collectives, on_device(): lax.all_to_all(coupling, 'wide', split_axis=3, concat_axis=1, tiled=True)  20.6 us
    all_gather x1, blocking collectives, on_device(): cells = lax.all_gather(re_cells, 'wide', axis=1, tiled=True)  9.04 us
    slice x1, local copies, waits for them, and re-layouts, on_device(): real = summed[:, 0, :, 0] - summed[:, 1, :, 1]  8.14 us
    unnamed x19, local copies, waits for them, and re-layouts  7.58 us
    reshape x1, local copies, waits for them, and re-layouts, on_device(): summed = summed.reshape(cell_count, 2, entries, 2, q_local)  6.59 us
    dot_general x1, matrix products, on_device(): lax.dot_general(lax.all_gather(flat, 'blk', axis=0, tiled=True), table, (...  6.53 us
    another operation x1, other arithmetic  4.24 us
  transfers between devices with their start and end apart: 1, of which 1 were waited for; matrix products, arithmetic and copies ran while one was open for 5% of the time, Pallas kernels for 0%

commit v1 on v0

--- a/solution.py
+++ b/solution.py
@@ -3,6 +3,7 @@
 import jax.numpy as jnp
 from jax import lax
 from jax.sharding import PartitionSpec as P
+from jax.lax import all_to_all, axis_size
 
 MODES = 16
 MESHQ = 32
@@ -33,7 +34,14 @@
     slab_rows = coupling.shape[0]
     q_local = q_points.shape[1]
     high = lax.Precision.HIGHEST
-    moved = lax.all_to_all(coupling, "wide", split_axis=3, concat_axis=1, tiled=True)
+
+    def load_record(s0):
+        placed = jnp.concatenate(
+            all_to_all(jnp.stack(jnp.split(s0, axis_size("wide"), axis=3)), "wide", 0, 0), axis=1
+        )
+        return placed
+
+    moved = load_record(coupling)
     cells = lax.all_gather(re_cells, "wide", axis=1, tiled=True)
     entries = moved.shape[3]
     offset = lax.axis_index("wide") * entries

time: 107 us -> 102 us (0.953)
  local copies, waits for them, and re-layouts: 24.1 us -> 15.5 us
  matrix products: 12 us -> 15.2 us
    unnamed x19 -> x16, local copies, waits for them, and re-layouts: 7.58 us -> 0.72 us
    slice x1, local copies, waits for them, and re-layouts: 8.14 us -> 6.56 us  [on_device(): real = summed[:, 0, :, 0] - summed[:, 1, :, 1]]
    split x0 -> x1, local copies, waits for them, and re-layouts: none -> 1.47 us  [load_record(): jnp.split(s0, axis_size('wide'), axis=3)]
    dot_general x1, matrix products: 0.99 us -> 2.08 us  [on_device(): jnp.einsum('kr,req->keq', k_cos, real, precision=high)]
    dot_general x1, matrix products: 1 us -> 2.09 us  [on_device(): jnp.einsum('kr,req->keq', k_sin, imag, precision=high)]
    dot_general x1, matrix products: 1 us -> 2.09 us  [on_device(): jnp.einsum('kr,req->keq', k_sin, real, precision=high)]
    another operation x1 -> x2, other arithmetic: 4.24 us -> 4.31 us
where the time goes in v1:
time: 102 us; the launch traced here: 101 us
  blocking collectives  29.8 us (29%)
  waiting for transfers between devices  22.4 us (22%)
  local copies, waits for them, and re-layouts  15.5 us (15%)
  matrix products  15.2 us (15%)
  between operations  13.6 us (13%)
  other arithmetic  4.98 us (5%)
    all_gather x1, waiting for transfers between devices, on_device(): lax.all_gather(flat, 'blk', axis=0, tiled=True)  22.4 us
    all_to_all x1, blocking collectives, load_record(): all_to_all(jnp.stack(jnp.split(s0, axis_size('wide'), axis=3)), 'wide', 0...  20.7 us
    all_gather x1, blocking collectives, on_device(): cells = lax.all_gather(re_cells, 'wide', axis=1, tiled=True)  9.04 us
    dot_general x1, matrix products, on_device(): lax.dot_general(lax.all_gather(flat, 'blk', axis=0, tiled=True), table, (...  6.59 us
    slice x1, local copies, waits for them, and re-layouts, on_device(): real = summed[:, 0, :, 0] - summed[:, 1, :, 1]  6.56 us
    reshape x1, local copies, waits for them, and re-layouts, on_device(): summed = summed.reshape(cell_count, 2, entries, 2, q_local)  5.88 us
    another operation x1, other arithmetic  4.24 us
    dot_general x1, matrix products, on_device(): jnp.einsum('kr,req->keq', k_sin, real, precision=high)  2.09 us
  transfers between devices with their start and end apart: 1, of which 1 were waited for; matrix products, arithmetic and copies ran while one was open for 5% of the time, Pallas kernels for 0%

profile of v1, /device:TPU:0, one launch (start us, length us, event | category | flops | bytes accessed | tf_op | source)
XLA Modules:
  0.0 101.4 jit_solution(10782819077773584544)
XLA Ops:
  6.5 0.0 all-gather.3.cloned.1.call-start
  6.6 1.5 %fusion.37 = (bf16[128,2,2,128]{3,2,1,0:T(2,128)(2,1)S(1)}, bf16[128,2,2,128]{3,2,1,0:T(2,128)(2,1)S(1)}, bf16[128,2,2,128]{3,2,1,0:T(2,128)(2,1)S(1)}, bf16[128,2,2,128]{3,2,1,0:T(2,128)(2,1)S(1)}) fusion(bf16[128,2,2,512]{3,2,1,0:T(2,128)(2,1)} %param.6), kind=kLoop, calls=%fused_computation.52 | loop fusion | bytes 1048576 | tf_op jit(solution)/shard_map/split | solution.py:40
  8.1 0.1 copy.47
  8.2 0.1 copy.48
  8.3 0.1 copy.49
  8.5 0.1 copy.50
  8.6 0.1 pad_maximum_fusion
  8.7 20.7 %all_to_all.5 = bf16[4,128,2,2,128]{1,4,3,2,0:T(8,128)(2,1)} all-to-all(bf16[4,128,2,2,128]{1,4,3,2,0:T(8,128)(2,1)S(1)} %pad_maximum_fusion), channel_id=1, replica_groups=mesh['blk'=8,'wide'=4] {'wide'}, dimensions={0} | all-to-all | bytes 1048576 | tf_op jit(solution)/shard_map/all_to_all | solution.py:40
  29.4 0.0 all-gather.3.cloned.1.call-update
  29.5 0.0 copy-done.3
  29.5 9.0 %all-gather = s32[4,2,3]{2,1,0:T(2,128)S(1)} all-gather(s32[1,2,3]{2,1,0:T(2,128)S(1)} %bitcast.46), channel_id=1, replica_groups=mesh['blk'=8,'wide'=4] {'wide'}, dimensions={0}, use_global_device_ids=true | all-gather | bytes 120 | tf_op jit(solution)/shard_map/all_gather | solution.py:45
  38.5 0.1 copy.37
  38.6 0.0 copy-done.4
  38.6 0.1 copy.36
  38.7 0.1 multiply_reduce_fusion.1
  38.8 0.1 fusion.34
  38.9 0.0 copy-done
  38.9 0.0 copy-done.2
  38.9 0.3 multiply_reduce_fusion
  39.2 0.0 copy-done.1
  39.2 0.3 fusion.19
  39.5 4.2 %cosine_convert_fusion = (bf16[256,1024]{1,0:T(8,128)(2,1)S(1)}, bf16[256,1024]{1,0:T(8,128)(2,1)S(1)}) fusion(s32[256,1024]{1,0:T(8,128)S(1)} %multiply_reduce_fusion), kind=kLoop, calls=%fused_computation.22 | loop fusion | flops 3932160 | bytes 2097152 | tf_op jit(solution)/shard_map/convert
  43.7 22.4 %all-gather.3.cloned.1.call-done = bf16[1024,2048]{0,1:T(8,128)(2,1)} async-done(((bf16[128,2048]{0,1:T(8,128)(2,1)}), bf16[1024,2048]{0,1:T(8,128)(2,1)}) %all-gather.3.cloned.1.call-update) | async-done | bytes 4194320 | tf_op jit(solution)/shard_map/all_gather | solution.py:52
  66.1 6.6 %fusion.5 = f32[2048,512]{1,0:T(8,128)} fusion(bf16[1024,2048]{0,1:T(8,128)(2,1)} %all-gather.3.cloned.1.call-done, bf16[256,1024]{1,0:T(8,128)(2,1)S(1)} %get-tuple-element.12, bf16[256,1024]{1,0:T(8,128)(2,1)S(1)} %get-tuple-element.11), kind=kOutput, calls=%fused_computation.11 | convolution fusion | flops 2149580800 | bytes 9437184 | tf_op jit(solution)/shard_map/dot_general | solution.py:51
  72.7 5.9 %reshape.29 = f32[8,2,128,2,256]{4,3,2,1,0:T(2,128)} reshape(f32[2048,512]{1,0:T(8,128)} %fusion.5) | data formatting | bytes 8388608 | tf_op jit(solution)/shard_map/reshape | solution.py:57
  78.5 6.6 %fusion.36 = (f32[8,1,128,1,256]{4,3,2,1,0:T(1,128)S(1)}, f32[8,1,128,1,256]{4,3,2,1,0:T(1,128)S(1)}, f32[8,1,128,1,256]{4,3,2,1,0:T(1,128)S(1)}, f32[8,1,128,1,256]{4,3,2,1,0:T(1,128)S(1)}) fusion(f32[8,2,128,2,256]{4,3,2,1,0:T(2,128)} %reshape.29), kind=kLoop, calls=%fused_computation.51 | loop fusion | bytes 8388608 | tf_op jit(solution)/shard_map/slice | solution.py:58
  85.1 2.1 %fusion.14 = f32[2,128,256]{2,0,1:T(2,128)S(1)} fusion(f32[8,1,128,1,256]{4,3,2,1,0:T(1,128)S(1)} %get-tuple-element.9, f32[8,1,128,1,256]{4,3,2,1,0:T(1,128)S(1)} %get-tuple-element.7, f32[128,256]{1,0:T(8,128)S(1)} %fusion.19, f32[2,8]{1,0:T(2,128)S(1)} %cos.6), kind=kOutput, calls=%fused_computation.25 | convolution fusion | flops 6815744 | bytes 2490432 | tf_op jit(solution)/shard_map/kr,req->keq/dot_general | solution.py:64
  87.2 2.1 %fusion.16 = f32[2,128,256]{2,0,1:T(2,128)S(1)} fusion(f32[8,1,128,1,256]{4,3,2,1,0:T(1,128)S(1)} %get-tuple-element.10, f32[8,1,128,1,256]{4,3,2,1,0:T(1,128)S(1)} %get-tuple-element.8, f32[128,256]{1,0:T(8,128)S(1)} %fusion.19, f32[2,8]{1,0:T(2,128)S(1)} %cos.6), kind=kOutput, calls=%fused_computation.26 | convolution fusion | flops 6815744 | bytes 2490432 | tf_op jit(solution)/shard_map/kr,req->keq/dot_general | solution.py:67
  89.3 2.1 %fusion.1 = f32[2,1,128,256]{3,0,2,1:T(2,128)S(1)} fusion(f32[2,128,256]{2,0,1:T(2,128)S(1)} %fusion.14, f32[8,1,128,1,256]{4,3,2,1,0:T(1,128)S(1)} %get-tuple-element.10, f32[8,1,128,1,256]{4,3,2,1,0:T(1,128)S(1)} %get-tuple-element.8, f32[128,256]{1,0:T(8,128)S(1)} %fusion.19, f32[2,8]{1,0:T(2,128)S(1)} %get-tuple-element.5), kind=kOutput, calls=%fused_computation.7 | convolution fusion | flops 6881280 | bytes 2752576 | tf_op jit(solution)/shard_map/kr,req->keq/dot_general | solution.py:64
  91.4 2.1 %fusion = f32[2,1,128,256]{3,0,2,1:T(2,128)S(1)} fusion(f32[2,128,256]{2,0,1:T(2,128)S(1)} %fusion.16, f32[8,1,128,1,256]{4,3,2,1,0:T(1,128)S(1)} %get-tuple-element.9, f32[8,1,128,1,256]{4,3,2,1,0:T(1,128)S(1)} %get-tuple-element.7, f32[128,256]{1,0:T(8,128)S(1)} %fusion.19, f32[2,8]{1,0:T(2,128)S(1)} %get-tuple-element.5), kind=kOutput, calls=%fused_computation.5 | convolution fusion | flops 6881280 | bytes 2752576 | tf_op jit(solution)/shard_map/kr,req->keq/dot_general | solution.py:67
  93.5 0.2 pad_maximum_fusion.1
  93.7 0.8 copy.46
  (7 shorter events, 0.1 us)
Async XLA Ops:
  6.5 22.9 %copy-start.3 = (s32[3,2]{0,1:T(2,128)S(1)}, s32[3,2]{0,1:T(2,128)}, u32[]{:S(2)}) copy-start(s32[3,2]{0,1:T(2,128)} %param.8) | copy-start | bytes 76
  6.5 32.1 %copy-start.4 = (s32[3,2]{0,1:T(2,128)S(1)}, s32[3,2]{0,1:T(2,128)}, u32[]{:S(2)}) copy-start(s32[3,2]{0,1:T(2,128)} %param.10) | copy-start | bytes 76
  6.5 32.3 %copy-start = (s32[3,1024]{1,0:T(4,128)S(1)}, s32[3,1024]{1,0:T(4,128)}, u32[]{:S(2)}) copy-start(s32[3,1024]{1,0:T(4,128)} %param.7) | copy-start | bytes 36868
  6.5 32.4 %copy-start.2 = (s32[3,256]{1,0:T(4,128)S(1)}, s32[3,256]{1,0:T(4,128)}, u32[]{:S(2)}) copy-start(s32[3,256]{1,0:T(4,128)} %param.9) | copy-start | bytes 9220
  6.5 32.7 %copy-start.1 = (f32[16,256]{1,0:T(8,128)S(1)}, f32[16,256]{1,0:T(8,128)}, u32[]{:S(2)}) copy-start(f32[16,256]{1,0:T(8,128)} %param.11) | copy-start | bytes 49156
  6.5 59.5 %all-gather.3.cloned.1.call-start = ((), (), s32[]{:S(2)}) async-start(), calls=%async_computation.1 | async-start | bytes 4718592 | tf_op jit(solution)/shard_map/all_gather | solution.py:52
Sparse Core Ops, SparseCore 0:
  29.6 36.4 all-gather.2
